TPU v7x, 32 devices: a whole 2x2x4 slice. The times are simulated.
32 devices in a mesh: grp: 2 (over x), tm: 16 (over z, y, core).
Axes of the slice: x: 2, y: 2, z: 4, core: 2. Of those that a mesh axis runs over, the one named last changes fastest.
Arguments:
- frames_in: bfloat16 [16384, 1536], P(('grp', 'tm')), parts along dimension 0, may hold values from -6 to 6
- frame_time: int32 [64], P('grp'), parts along dimension 0, may hold values from 0 to 31, each once
- norm_gain: float32 [1536], replicated, may hold values from 0.25 to 1.75
- w_query: bfloat16 [1536, 768], replicated, may hold values from -2 to 2
- w_key: bfloat16 [1536, 768], replicated, may hold values from -2 to 2
- w_value: bfloat16 [1536, 768], replicated, may hold values from -0.15625 to 0.15625
- w_output: bfloat16 [768, 1536], replicated, may hold values from -0.21875 to 0.21875
Outputs:
- attended: bfloat16 [16384, 1536], P(('grp', 'tm')), parts along dimension 0
There are 2 independent parts, one for each index of `grp`. A program takes and returns all parts, laid end to end along the dimension named above; an argument that names none is the same for every part. Nothing has to cross between parts.
Inputs may be any that keep to these rules, and one draw needn't show every extreme that they name: `frame_time`: each of 0 to 31 stands once.
All inputs are finite; a program needn't handle non-finite values.
Results may differ from a plain program's by a relative error of at most 0.004.
The roundings to bfloat16 on the way count: a program that leaves them out, or rounds other values in their place, can miss the bound.
Values may be sent and summed in bfloat16 or wider, within the bound.
A program may use at most 128 MiB of HBM per device.

v0:
```python
import jax
import jax.numpy as jnp
from jax import lax
from jax.sharding import PartitionSpec as P

HEADS = 6
HD = 128
HH = 16
WW = 16
WIN = 8
POOL = 4


def normed_rows(frames_in, norm_gain):
    values_f = frames_in.astype(jnp.float32)
    scale = lax.rsqrt(jnp.mean(values_f * values_f, axis=-1, keepdims=True) + 1e-06)
    return (values_f * scale * norm_gain).astype(jnp.bfloat16)


def to_windows(array, count):
    shaped = array.reshape(count, HH // WIN, WIN, WW // WIN, WIN, HEADS, HD)
    shaped = shaped.transpose(0, 1, 3, 2, 4, 5, 6)
    return shaped.reshape(count, HH // WIN * (WW // WIN), WIN * WIN, HEADS, HD)


def from_windows(array, count):
    shaped = array.reshape(count, HH // WIN, WW // WIN, WIN, WIN, HEADS * HD)
    shaped = shaped.transpose(0, 1, 3, 2, 4, 5)
    return shaped.reshape(count * HH * WW, HEADS * HD)


def pooled(array, count):
    pool_rows = HH // POOL * (WW // POOL)
    shaped = array.reshape(count, HH // POOL, POOL, WW // POOL, POOL, HEADS * HD).astype(
        jnp.float32
    )
    return jnp.mean(shaped, axis=(2, 4)).reshape(count * pool_rows, HEADS * HD).astype(jnp.bfloat16)


def on_device(frames_in, frame_time, norm_gain, w_query, w_key, w_value, w_output):
    count = frames_in.shape[0] // (HH * WW)
    pool_rows = HH // POOL * (WW // POOL)
    all_frames = frame_time.shape[0]
    normed = normed_rows(frames_in, norm_gain)
    query = jnp.dot(normed, w_query, preferred_element_type=jnp.float32).astype(jnp.bfloat16)
    keys = jnp.dot(normed, w_key, preferred_element_type=jnp.float32).astype(jnp.bfloat16)
    values = jnp.dot(normed, w_value, preferred_element_type=jnp.float32).astype(jnp.bfloat16)
    pooled_keys = pooled(keys, count)
    pooled_values = pooled(values, count)
    own_time = lax.dynamic_slice_in_dim(frame_time, lax.axis_index("tm") * count, count)
    query_win = to_windows(query, count)
    factor = 1.0 / HD**0.5
    local_s = (
        jnp.einsum(
            "fnqhd,fnkhd->fnhqk",
            query_win,
            to_windows(keys, count),
            preferred_element_type=jnp.float32,
        )
        * factor
    )
    top = jnp.max(local_s, -1)
    local_w = jnp.exp(local_s - top[..., None])
    local_acc = jnp.einsum(
        "fnhqk,fnkhd->fnhqd",
        local_w.astype(jnp.bfloat16),
        to_windows(values, count),
        preferred_element_type=jnp.float32,
    )
    whole_keys, whole_values = (
        lax.all_gather(pooled_keys, "tm", axis=0, tiled=True),
        lax.all_gather(pooled_values, "tm", axis=0, tiled=True),
    )
    rows = whole_keys.shape[0]
    slot = jnp.arange(rows, dtype=jnp.int32) // pool_rows
    match = slot[:, None] == jnp.arange(all_frames, dtype=jnp.int32)[None, :]
    key_time = jnp.sum(jnp.where(match, frame_time[None, :], 0), axis=1)
    best = top
    total = jnp.sum(local_w, -1)
    acc = local_acc
    scores = (
        jnp.einsum(
            "fnqhd,khd->fnhqk",
            query_win,
            whole_keys.reshape(rows, HEADS, HD),
            preferred_element_type=jnp.float32,
        )
        * factor
    )
    valid = (key_time[None, :] < own_time[:, None])[:, None, None, None, :]
    scores = jnp.where(valid, scores, -1e30)
    new_best = jnp.maximum(best, jnp.max(scores, -1))
    keep = jnp.exp(best - new_best)
    weights = jnp.where(valid, jnp.exp(scores - new_best[..., None]), 0.0)
    total = total * keep + jnp.sum(weights, -1)
    acc = acc * keep[..., None] + jnp.einsum(
        "fnhqk,khd->fnhqd",
        weights.astype(jnp.bfloat16),
        whole_values.reshape(rows, HEADS, HD),
        preferred_element_type=jnp.float32,
    )
    final = (new_best, total, acc)
    best, total, acc = final
    mixed = (acc / total[..., None]).transpose(0, 1, 3, 2, 4).astype(jnp.bfloat16)
    mixed = from_windows(mixed, count)
    return jnp.dot(mixed, w_output, preferred_element_type=jnp.float32).astype(jnp.bfloat16)


def solution(mesh):
    placed = (P(("grp", "tm"), None), P("grp"), P(), P(), P(), P(), P())
    return jax.shard_map(
        on_device, mesh=mesh, in_specs=placed, out_specs=P(("grp", "tm"), None), check_vma=False
    )
```

profile of v0, /device:TPU:0, one launch (start us, length us, event | category | flops | bytes accessed | tf_op | source)
XLA Modules:
  0.0 85.4 jit_solution(2821864571280386767)
XLA Ops:
  0.0 0.9 %dynamic_slice.3 = s32[2]{0:T(128)S(1)} dynamic-slice(s32[32]{0:T(128)} %param.8, s32[]{:T(128)S(6)} %select_n.25), dynamic_slice_sizes={2} | dynamic-slice | bytes 20 | tf_op jit(solution)/shard_map/dynamic_slice | solution.py:50
  0.9 0.7 select_reduce_fusion
  1.7 1.8 %fusion.3 = f32[512]{0:T(512)S(1)} fusion(bf16[512,1536]{1,0:T(8,128)(2,1)} %param.7), kind=kLoop, calls=%fused_computation.7 | loop fusion | flops 2358784 | bytes 1574912 | tf_op jit(solution)/shard_map/reduce_sum | solution.py:16
  3.5 3.6 %convolution_convert_fusion.2 = bf16[512,768]{1,0:T(8,128)(2,1)S(1)} fusion(bf16[1536,768]{1,0:T(8,128)(2,1)} %param.11, bf16[512,1536]{1,0:T(8,128)(2,1)} %param.7, f32[1536]{0:T(1024)} %param.9, f32[512]{0:T(512)S(1)} %add_rsqrt_fusion), kind=kOutput, calls=%fused_computation.20 | convolution fusion | flops 1211498496 | bytes 4726784 | tf_op jit(solution)/shard_map/dot_general | solution.py:46
  7.1 1.5 %reshape.124 = f32[2,4,4,4,4,768]{5,4,3,2,1,0:T(4,128)} reshape(bf16[512,768]{1,0:T(8,128)(2,1)S(1)} %convolution_convert_fusion.2) | data formatting | bytes 2359296 | tf_op jit(solution)/shard_map/convert_element_type | solution.py:34
  8.6 1.9 %reduce_sum.60 = f32[2,4,4,768]{3,2,1,0:T(4,128)S(1)} reduce(f32[2,4,4,4,4,768]{5,4,3,2,1,0:T(4,128)} %reshape.124, f32[]{:T(128)} %constant.15.clone.1), dimensions={2,4}, to_apply=%region_3.0 | reduce | flops 368640 | bytes 1671172 | tf_op jit(solution)/shard_map/reduce_sum | solution.py:37
  10.6 26.7 %all_gather.6 = bf16[512,768]{1,0:T(8,128)(2,1)} all-gather(bf16[32,768]{1,0:T(8,128)(2,1)S(1)} %convert_element_type.60), channel_id=1, replica_groups=mesh['grp'=2,'tm'=16] {'tm'}, dimensions={0}, use_global_device_ids=true | all-gather | bytes 835584 | tf_op jit(solution)/shard_map/all_gather | solution.py:71
  37.3 1.4 %copy.75 = bf16[512,768]{0,1:T(8,128)(2,1)S(1)} copy(bf16[512,768]{1,0:T(8,128)(2,1)} %all_gather.6) | data formatting | bytes 1572864 | tf_op jit(solution)/shard_map/all_gather | solution.py:71
  38.8 3.6 %convolution_convert_fusion.3 = bf16[512,768]{1,0:T(8,128)(2,1)S(1)} fusion(bf16[1536,768]{1,0:T(8,128)(2,1)} %param.10, bf16[512,1536]{1,0:T(8,128)(2,1)} %param.7, f32[1536]{0:T(1024)S(1)} %copy-done.9, f32[512]{0:T(512)S(1)} %add_rsqrt_fusion), kind=kOutput, calls=%fused_computation.21 | convolution fusion | flops 1211498496 | bytes 4726784 | tf_op jit(solution)/shard_map/dot_general | solution.py:45
  42.6 1.1 %fusion = (f32[2,4,6,64]{3,1,0,2:T(4,128)S(1)}, f32[6,512,2,4,64]{1,4,3,2,0:T(8,128)S(1)}) fusion(pred[2,512]{1,0:T(4,128)(4,1)S(1)} %broadcast_compare_fusion, bf16[512,6,128,1,1]{0,2,4,3,1:T(8,128)(2,1)S(1)} %bitcast.70, bf16[2,4,64,6,128]{4,2,1,0,3:T(8,128)(2,1)S(1)} %bitcast.68), kind=kOutput, calls=%fused_computation.2 | convolution fusion | flops 407368704 | bytes 7877632 | tf_op jit(solution)/shard_map/fnqhd,khd->fnhqk/dot_general | solution.py:82
  43.9 0.6 fusion.23
  44.6 3.1 %fusion.1 = (f32[2,4,6,64]{3,1,0,2:T(4,128)S(1)}, bf16[2,4,6,64,512]{4,3,1,0,2:T(8,128)(2,1)}) fusion(f32[6,512,2,4,64]{1,4,3,2,0:T(8,128)S(1)} %get-tuple-element.12, f32[2,4,6,64]{3,1,0,2:T(4,128)S(1)} %copy.80, pred[2,512]{1,0:T(4,128)(4,1)S(1)} %broadcast_compare_fusion), kind=kLoop, calls=%fused_computation.3 | loop fusion | flops 9434112 | bytes 9462784 | tf_op jit(solution)/shard_map/reduce_sum | solution.py:95
  47.7 0.4 fusion.10
  48.4 1.5 %convolution_convert_fusion.1 = bf16[512,768]{1,0:T(8,128)(2,1)S(1)} fusion(bf16[1536,768]{1,0:T(8,128)(2,1)S(1)} %copy-done.8, bf16[512,1536]{1,0:T(8,128)(2,1)S(1)} %copy-done.7, f32[1536]{0:T(1024)S(1)} %copy-done.9, f32[512]{0:T(512)S(1)} %add_rsqrt_fusion), kind=kOutput, calls=%fused_computation.19 | convolution fusion | flops 1211498496 | bytes 4726784 | tf_op jit(solution)/shard_map/dot_general | solution.py:47
  49.9 1.5 %reshape.125 = f32[2,4,4,4,4,768]{5,4,3,2,1,0:T(4,128)} reshape(bf16[512,768]{1,0:T(8,128)(2,1)S(1)} %convolution_convert_fusion.1) | data formatting | bytes 2359296 | tf_op jit(solution)/shard_map/convert_element_type | solution.py:34
  51.4 1.9 %reduce_sum.61 = f32[2,4,4,768]{3,2,1,0:T(4,128)S(1)} reduce(f32[2,4,4,4,4,768]{5,4,3,2,1,0:T(4,128)} %reshape.125, f32[]{:T(128)} %constant.15.clone.1), dimensions={2,4}, to_apply=%region_5.6 | reduce | flops 368640 | bytes 1671172 | tf_op jit(solution)/shard_map/reduce_sum | solution.py:37
  53.4 19.8 %all_gather.7 = bf16[512,768]{1,0:T(8,128)(2,1)S(1)} all-gather(bf16[32,768]{1,0:T(8,128)(2,1)S(1)} %convert_element_type.64), channel_id=1, replica_groups=mesh['grp'=2,'tm'=16] {'tm'}, dimensions={0}, use_global_device_ids=true | all-gather | bytes 835584 | tf_op jit(solution)/shard_map/all_gather | solution.py:72
  73.1 1.2 %copy.78 = bf16[512,768]{0,1:T(8,128)(2,1)} copy(bf16[512,768]{1,0:T(8,128)(2,1)S(1)} %all_gather.7) | data formatting | bytes 1572864 | tf_op jit(solution)/shard_map/all_gather | solution.py:72
  74.3 3.3 %fusion.6 = f32[6,128,2,4,64]{1,4,0,3,2:T(8,128)S(1)} fusion(bf16[512,6,128,1,1]{0,2,1,4,3:T(8,128)(2,1)} %bitcast.76, bf16[2,4,6,64,512]{4,3,1,0,2:T(8,128)(2,1)} %get-tuple-element.8), kind=kOutput, calls=%fused_computation.10 | convolution fusion | flops 402653184 | bytes 5505024 | tf_op jit(solution)/shard_map/fnhqk,khd->fnhqd/dot_general | solution.py:96
  77.8 1.5 %fusion.9 = bf16[2,4,64,6,128]{4,2,3,1,0:T(8,128)(2,1)S(1)} fusion(f32[6,128,2,4,64]{1,4,0,3,2:T(8,128)S(1)} %fusion.6, bf16[2,4,64,6,128]{4,2,3,1,0:T(8,128)(2,1)S(1)} %bitcast.75, f32[2,4,6,64,64]{3,4,2,1,0:T(8,128)S(1)} %copy-done.2, f32[2,4,64,6]{2,3,1,0:T(8,128)S(1)} %get-tuple-element.5, f32[2,4,64,6]{2,3,1,0:T(8,128)S(1)} %get-tuple-element.6, ...), kind=kOutput, calls=%fused_computation.15 | convolution fusion | flops 52297728 | bytes 3969024 | tf_op jit(solution)/shard_map/fnhqk,fnkhd->fnhqd/dot_general | solution.py:64
  79.3 0.6 copy.84
  79.8 1.8 %reshape.122 = bf16[2,2,2,8,8,768]{5,4,3,2,1,0:T(8,128)(2,1)} reshape(bf16[2,4,64,6,128]{4,3,2,1,0:T(8,128)(2,1)S(1)} %copy.84) | data formatting | bytes 1572864 | tf_op jit(solution)/shard_map/reshape | solution.py:27
  81.6 1.2 %copy.85 = bf16[2,2,8,2,8,768]{5,4,3,2,1,0:T(8,128)(2,1)S(1)} copy(bf16[2,2,8,2,8,768]{5,4,2,3,1,0:T(8,128)(2,1)} %bitcast.71) | data formatting | bytes 1572864 | tf_op jit(solution)/shard_map/transpose | solution.py:28
  82.8 2.5 %convolution_convert_fusion = bf16[512,1536]{1,0:T(8,128)(2,1)} fusion(bf16[512,768]{1,0:T(8,128)(2,1)S(1)} %bitcast.77, bf16[768,1536]{1,0:T(8,128)(2,1)S(1)} %copy-done), kind=kOutput, calls=%fused_computation.12 | convolution fusion | flops 1208745984 | bytes 4718592 | tf_op jit(solution)/shard_map/dot_general | solution.py:106
  (33 shorter events, 1.2 us)
Async XLA Ops:
  0.0 82.8 %copy-start = (bf16[768,1536]{1,0:T(8,128)(2,1)S(1)}, bf16[768,1536]{1,0:T(8,128)(2,1)}, u32[]{:S(2)}) copy-start(bf16[768,1536]{1,0:T(8,128)(2,1)} %param.13) | copy-start | bytes 7077892
  7.1 3.5 %copy-start.3 = (bf16[512,768]{1,0:T(8,128)(2,1)}, bf16[512,768]{1,0:T(8,128)(2,1)S(1)}, u32[]{:S(2)}) copy-start(bf16[512,768]{1,0:T(8,128)(2,1)S(1)} %convolution_convert_fusion.2) | copy-start | bytes 2359300
  8.6 30.1 %copy-start.9 = (f32[1536]{0:T(1024)S(1)}, f32[1536]{0:T(1024)}, u32[]{:S(2)}) copy-start(f32[1536]{0:T(1024)} %param.9) | copy-start | bytes 18436
  42.6 1.1 %copy-start.4 = (bf16[512,768]{1,0:T(8,128)(2,1)S(1)}, bf16[512,768]{1,0:T(8,128)(2,1)}, u32[]{:S(2)}) copy-start(bf16[512,768]{1,0:T(8,128)(2,1)} %copy-done.3) | copy-start | bytes 2359300
  44.5 3.2 %copy-start.1 = (f32[2,4,6,64,64]{3,4,2,1,0:T(8,128)}, f32[2,4,6,64,64]{3,4,2,1,0:T(8,128)S(1)}, u32[]{:S(2)}) copy-start(f32[2,4,6,64,64]{3,4,2,1,0:T(8,128)S(1)} %get-tuple-element.10) | copy-start | bytes 2359300
  44.6 3.6 %copy-start.7 = (bf16[512,1536]{1,0:T(8,128)(2,1)S(1)}, bf16[512,1536]{1,0:T(8,128)(2,1)}, u32[]{:S(2)}) copy-start(bf16[512,1536]{1,0:T(8,128)(2,1)} %param.7) | copy-start | bytes 4718596
  44.6 3.8 %copy-start.8 = (bf16[1536,768]{1,0:T(8,128)(2,1)S(1)}, bf16[1536,768]{1,0:T(8,128)(2,1)}, u32[]{:S(2)}) copy-start(bf16[1536,768]{1,0:T(8,128)(2,1)} %param.12) | copy-start | bytes 7077892
  49.9 3.5 %copy-start.5 = (bf16[512,768]{1,0:T(8,128)(2,1)}, bf16[512,768]{1,0:T(8,128)(2,1)S(1)}, u32[]{:S(2)}) copy-start(bf16[512,768]{1,0:T(8,128)(2,1)S(1)} %convolution_convert_fusion.1) | copy-start | bytes 2359300
  74.3 3.3 %copy-start.6 = (bf16[512,768]{1,0:T(8,128)(2,1)S(1)}, bf16[512,768]{1,0:T(8,128)(2,1)}, u32[]{:S(2)}) copy-start(bf16[512,768]{1,0:T(8,128)(2,1)} %copy-done.5) | copy-start | bytes 2359300
  74.3 3.5 %copy-start.2 = (f32[2,4,6,64,64]{3,4,2,1,0:T(8,128)S(1)}, f32[2,4,6,64,64]{3,4,2,1,0:T(8,128)}, u32[]{:S(2)}) copy-start(f32[2,4,6,64,64]{3,4,2,1,0:T(8,128)} %copy-done.1) | copy-start | bytes 2359300
where the time goes:
time: 85.7 us; the launch traced here: 85.4 us
  blocking collectives  46.5 us (54%)
  matrix products  17.6 us (21%)
  local copies, waits for them, and re-layouts  11 us (13%)
  other arithmetic  9.99 us (12%)
    all_gather x1, blocking collectives, on_device(): lax.all_gather(pooled_keys, 'tm', axis=0, tiled=True)  26.7 us
    all_gather x1, blocking collectives, on_device(): lax.all_gather(pooled_values, 'tm', axis=0, tiled=True)  19.8 us
    reduce_sum x2, other arithmetic, pooled(): jnp.mean(shaped, axis=(2, 4)).reshape(count * pool_rows, HEADS * HD)  3.78 us
    dot_general x1, matrix products, on_device(): jnp.dot(normed, w_key, preferred_element_type=jnp.float32)  3.6 us
    dot_general x1, matrix products, on_device(): jnp.dot(normed, w_query, preferred_element_type=jnp.float32)  3.58 us
    dot_general x1, matrix products, on_device(): jnp.einsum('fnhqk,khd->fnhqd', weights.astype(jnp.bfloat16), whole_values...  3.25 us
    reduce_sum x1, other arithmetic, on_device(): total = total * keep + jnp.sum(weights, -1)  3.13 us
    convert_element_type x2, local copies, waits for them, and re-layouts, pooled(): array.reshape(count, HH // POOL, POOL, WW // POOL, POOL, HEADS * HD)  3.03 us

commit v1 on v0

--- a/solution.py
+++ b/solution.py
@@ -9,6 +9,16 @@
 WW = 16
 WIN = 8
 POOL = 4
+
+
+def collect(x, axis, dim):
+    ways, here, lap = (lax.axis_size(axis), lax.axis_index(axis), x.shape[dim])
+    shape = [n * ways if d == dim else n for d, n in enumerate(x.shape)]
+    full = lax.dynamic_update_slice_in_dim(jnp.zeros(shape, x.dtype), x, here * lap, axis=dim)
+    for far in range(1, ways):
+        x = lax.ppermute(x, axis, [(d, (d + 1) % ways) for d in range(ways)])
+        full = lax.dynamic_update_slice_in_dim(full, x, (here - far) % ways * lap, axis=dim)
+    return full
 
 
 def normed_rows(frames_in, norm_gain):
@@ -69,7 +79,7 @@
     )
     whole_keys, whole_values = (
         lax.all_gather(pooled_keys, "tm", axis=0, tiled=True),
-        lax.all_gather(pooled_values, "tm", axis=0, tiled=True),
+        collect(pooled_values, "tm", 0),
     )
     rows = whole_keys.shape[0]
     slot = jnp.arange(rows, dtype=jnp.int32) // pool_rows

time: 85.7 us -> 172 us (2.01)
  waiting for transfers between devices: 0 us -> 58.5 us
  local copies, waits for them, and re-layouts: 11 us -> 59.4 us
  blocking collectives: 46.5 us -> 21.5 us
  matrix products: 17.6 us -> 20.7 us
    ppermute x0 -> x15, waiting for transfers between devices: none -> 58.5 us  [collect(): x = lax.ppermute(x, axis, [(d, (d + 1) % ways) for d in range(ways)])]
    dynamic_update_slice x0 -> x16, local copies, waits for them, and re-layouts: none -> 41 us  [the longest x15 38.8 us: collect(): lax.dynamic_update_slice_in_dim(full, x, (here - far) % ways * lap, axis=...]
    all_gather x1 -> x0, blocking collectives: 19.8 us -> none  [on_device(): lax.all_gather(pooled_values, 'tm', axis=0, tiled=True)]
    ppermute x0 -> x15, local copies, waits for them, and re-layouts: none -> 7.24 us  [collect(): x = lax.ppermute(x, axis, [(d, (d + 1) % ways) for d in range(ways)])]
    all_gather x1, blocking collectives: 26.7 us -> 21.5 us  [on_device(): lax.all_gather(pooled_keys, 'tm', axis=0, tiled=True)]
    dot_general x1, matrix products: 1.47 us -> 3.6 us  [on_device(): jnp.dot(normed, w_value, preferred_element_type=jnp.float32)]
  transfers between devices with their start and end apart: 0 -> 15, of which waited for: 0 -> 13; matrix products, arithmetic and copies ran while one was open for 0% -> 40% of each run, Pallas kernels for 0% -> 0%
where the time goes in v1:
time: 172 us
  local copies, waits for them, and re-layouts  59.4 us (35%)
  waiting for transfers between devices  58.5 us (34%)
  blocking collectives  21.5 us (12%)
  matrix products  20.7 us (12%)
  other arithmetic  10.1 us (6%)
    ppermute x15, waiting for transfers between devices, collect(): x = lax.ppermute(x, axis, [(d, (d + 1) % ways) for d in range(ways)])  58.5 us
    dynamic_update_slice x15, local copies, waits for them, and re-layouts, collect(): lax.dynamic_update_slice_in_dim(full, x, (here - far) % ways * lap, axis=...  38.8 us
    all_gather x1, blocking collectives, on_device(): lax.all_gather(pooled_keys, 'tm', axis=0, tiled=True)  21.5 us
    ppermute x15, local copies, waits for them, and re-layouts, collect(): x = lax.ppermute(x, axis, [(d, (d + 1) % ways) for d in range(ways)])  7.24 us
    dot_general x1, matrix products, on_device(): jnp.dot(normed, w_key, preferred_element_type=jnp.float32)  4.48 us
    reduce_sum x2, other arithmetic, pooled(): jnp.mean(shaped, axis=(2, 4)).reshape(count * pool_rows, HEADS * HD)  3.78 us
    dot_general x1, matrix products, on_device(): jnp.dot(normed, w_value, preferred_element_type=jnp.float32)  3.6 us
  transfers between devices with their start and end apart: 15, of which 13 were waited for; matrix products, arithmetic and copies ran while one was open for 40% of the time, Pallas kernels for 0%

profile of v1, /device:TPU:0, one launch (start us, length us, event | category | flops | bytes accessed | tf_op | source)
XLA Modules:
  0.0 171.6 jit_solution(8869464249306836666)
XLA Ops:
  2.0 3.6 %convolution_convert_fusion.1 = bf16[512,768]{1,0:T(8,128)(2,1)S(1)} fusion(bf16[1536,768]{1,0:T(8,128)(2,1)} %param.12, bf16[512,1536]{1,0:T(8,128)(2,1)} %param.7, f32[1536]{0:T(1024)} %param.9, f32[512]{0:T(512)S(1)} %add_rsqrt_fusion), kind=kOutput, calls=%fused_computation.19 | convolution fusion | flops 1211498496 | bytes 4726784 | tf_op jit(solution)/shard_map/dot_general | solution.py:57
  9.6 6.8 %collective-permute-done = bf16[32,768]{1,0:T(8,128)(2,1)S(1)} collective-permute-done((bf16[32,768]{1,0:T(8,128)(2,1)S(1)}, bf16[32,768]{1,0:T(8,128)(2,1)S(1)}, u32[]{:S(2)}, u32[]{:S(2)}) %collective-permute-start) | collective-permute-done | bytes 49184 | tf_op jit(solution)/shard_map/ppermute | solution.py:19
  16.4 4.5 %convolution_convert_fusion.2 = bf16[512,768]{1,0:T(8,128)(2,1)} fusion(bf16[1536,768]{1,0:T(8,128)(2,1)} %param.11, bf16[512,1536]{1,0:T(8,128)(2,1)} %param.7, f32[1536]{0:T(1024)S(1)} %copy-done.26, f32[512]{0:T(512)S(1)} %add_rsqrt_fusion), kind=kOutput, calls=%fused_computation.20 | convolution fusion | flops 1211498496 | bytes 4726784 | tf_op jit(solution)/shard_map/dot_general | solution.py:56
  28.9 6.2 %collective-permute-done.3 = bf16[32,768]{1,0:T(8,128)(2,1)S(1)} collective-permute-done((bf16[32,768]{1,0:T(8,128)(2,1)S(1)}, bf16[32,768]{1,0:T(8,128)(2,1)S(1)}, u32[]{:S(2)}, u32[]{:S(2)}) %collective-permute-start.3) | collective-permute-done | bytes 49184 | tf_op jit(solution)/shard_map/ppermute | solution.py:19
  35.0 21.5 %all_gather.3 = bf16[512,768]{1,0:T(8,128)(2,1)} all-gather(bf16[32,768]{1,0:T(8,128)(2,1)S(1)} %convert_element_type.60), channel_id=1, replica_groups=mesh['grp'=2,'tm'=16] {'tm'}, dimensions={0}, use_global_device_ids=true | all-gather | bytes 835584 | tf_op jit(solution)/shard_map/all_gather | solution.py:81
  56.7 6.0 %collective-permute-done.5 = bf16[32,768]{1,0:T(8,128)(2,1)S(1)} collective-permute-done((bf16[32,768]{1,0:T(8,128)(2,1)S(1)}, bf16[32,768]{1,0:T(8,128)(2,1)S(1)}, u32[]{:S(2)}, u32[]{:S(2)}) %collective-permute-start.5) | collective-permute-done | bytes 49184 | tf_op jit(solution)/shard_map/ppermute | solution.py:19
  62.9 6.0 %collective-permute-done.6 = bf16[32,768]{1,0:T(8,128)(2,1)S(1)} collective-permute-done((bf16[32,768]{1,0:T(8,128)(2,1)S(1)}, bf16[32,768]{1,0:T(8,128)(2,1)S(1)}, u32[]{:S(2)}, u32[]{:S(2)}) %collective-permute-start.6) | collective-permute-done | bytes 49184 | tf_op jit(solution)/shard_map/ppermute | solution.py:19
  77.8 3.7 %collective-permute-done.8 = bf16[32,768]{1,0:T(8,128)(2,1)S(1)} collective-permute-done((bf16[32,768]{1,0:T(8,128)(2,1)S(1)}, bf16[32,768]{1,0:T(8,128)(2,1)S(1)}, u32[]{:S(2)}, u32[]{:S(2)}) %collective-permute-start.8) | collective-permute-done | bytes 49184 | tf_op jit(solution)/shard_map/ppermute | solution.py:19
  82.0 5.7 %collective-permute-done.9 = bf16[32,768]{1,0:T(8,128)(2,1)S(1)} collective-permute-done((bf16[32,768]{1,0:T(8,128)(2,1)S(1)}, bf16[32,768]{1,0:T(8,128)(2,1)S(1)}, u32[]{:S(2)}, u32[]{:S(2)}) %collective-permute-start.9) | collective-permute-done | bytes 49184 | tf_op jit(solution)/shard_map/ppermute | solution.py:19
  87.7 6.2 %collective-permute-done.10 = bf16[32,768]{1,0:T(8,128)(2,1)S(1)} collective-permute-done((bf16[32,768]{1,0:T(8,128)(2,1)S(1)}, bf16[32,768]{1,0:T(8,128)(2,1)S(1)}, u32[]{:S(2)}, u32[]{:S(2)}) %collective-permute-start.10) | collective-permute-done | bytes 49184 | tf_op jit(solution)/shard_map/ppermute | solution.py:19
  93.9 3.1 %fusion.1 = (f32[2,4,6,64]{3,1,0,2:T(4,128)S(1)}, bf16[2,4,6,64,512]{4,3,1,0,2:T(8,128)(2,1)}) fusion(f32[6,512,2,4,64]{1,4,3,2,0:T(8,128)S(1)} %get-tuple-element.12, f32[2,4,6,64]{3,1,0,2:T(4,128)S(1)} %copy.140, pred[2,512]{1,0:T(4,128)(4,1)S(1)} %broadcast_compare_fusion), kind=kLoop, calls=%fused_computation.3 | loop fusion | flops 9434112 | bytes 9462784 | tf_op jit(solution)/shard_map/reduce_sum | solution.py:105
  97.2 2.8 %collective-permute-done.11 = bf16[32,768]{1,0:T(8,128)(2,1)S(1)} collective-permute-done((bf16[32,768]{1,0:T(8,128)(2,1)S(1)}, bf16[32,768]{1,0:T(8,128)(2,1)S(1)}, u32[]{:S(2)}, u32[]{:S(2)}) %collective-permute-start.11) | collective-permute-done | bytes 49184 | tf_op jit(solution)/shard_map/ppermute | solution.py:19
  101.7 4.6 %collective-permute-done.12 = bf16[32,768]{1,0:T(8,128)(2,1)S(1)} collective-permute-done((bf16[32,768]{1,0:T(8,128)(2,1)S(1)}, bf16[32,768]{1,0:T(8,128)(2,1)S(1)}, u32[]{:S(2)}, u32[]{:S(2)}) %collective-permute-start.12) | collective-permute-done | bytes 49184 | tf_op jit(solution)/shard_map/ppermute | solution.py:19
  106.7 5.9 %collective-permute-done.13 = bf16[32,768]{1,0:T(8,128)(2,1)} collective-permute-done((bf16[32,768]{1,0:T(8,128)(2,1)S(1)}, bf16[32,768]{1,0:T(8,128)(2,1)}, u32[]{:S(2)}, u32[]{:S(2)}) %collective-permute-start.13) | collective-permute-done | bytes 49184 | tf_op jit(solution)/shard_map/ppermute | solution.py:19
  127.1 2.9 %dynamic_update_slice.53 = bf16[512,768]{0,1:T(8,128)(2,1)S(1)} dynamic-update-slice(bf16[512,768]{0,1:T(8,128)(2,1)S(1)} %dynamic_update_slice.52, bf16[32,768]{0,1:T(8,128)(2,1)S(1)} %copy.128, s32[]{:T(128)S(6)} %select_n.148, s32[]{:T(128)} %constant.133.clone.1) | dynamic-update-slice | bytes 98308 | tf_op jit(solution)/shard_map/dynamic_update_slice | solution.py:20
  130.9 2.9 %dynamic_update_slice.54 = bf16[512,768]{0,1:T(8,128)(2,1)S(1)} dynamic-update-slice(bf16[512,768]{0,1:T(8,128)(2,1)S(1)} %dynamic_update_slice.53, bf16[32,768]{0,1:T(8,128)(2,1)S(1)} %copy.129, s32[]{:T(128)S(6)} %select_n.150, s32[]{:T(128)} %constant.133.clone.1) | dynamic-update-slice | bytes 98308 | tf_op jit(solution)/shard_map/dynamic_update_slice | solution.py:20
  134.0 2.9 %dynamic_update_slice.55 = bf16[512,768]{0,1:T(8,128)(2,1)S(1)} dynamic-update-slice(bf16[512,768]{0,1:T(8,128)(2,1)S(1)} %dynamic_update_slice.54, bf16[32,768]{0,1:T(8,128)(2,1)S(1)} %copy.130, s32[]{:T(128)S(6)} %select_n.152, s32[]{:T(128)} %constant.133.clone.1) | dynamic-update-slice | bytes 98308 | tf_op jit(solution)/shard_map/dynamic_update_slice | solution.py:20
  139.2 2.9 %dynamic_update_slice.57 = bf16[512,768]{0,1:T(8,128)(2,1)S(1)} dynamic-update-slice(bf16[512,768]{0,1:T(8,128)(2,1)S(1)} %dynamic_update_slice.56, bf16[32,768]{0,1:T(8,128)(2,1)S(1)} %copy.132, s32[]{:T(128)S(6)} %select_n.156, s32[]{:T(128)} %constant.133.clone.1) | dynamic-update-slice | bytes 98308 | tf_op jit(solution)/shard_map/dynamic_update_slice | solution.py:20
  142.3 2.9 %dynamic_update_slice.58 = bf16[512,768]{0,1:T(8,128)(2,1)S(1)} dynamic-update-slice(bf16[512,768]{0,1:T(8,128)(2,1)S(1)} %dynamic_update_slice.57, bf16[32,768]{0,1:T(8,128)(2,1)S(1)} %copy.133, s32[]{:T(128)S(6)} %select_n.158, s32[]{:T(128)} %constant.133.clone.1) | dynamic-update-slice | bytes 98308 | tf_op jit(solution)/shard_map/dynamic_update_slice | solution.py:20
  146.1 2.9 %dynamic_update_slice.59 = bf16[512,768]{0,1:T(8,128)(2,1)S(1)} dynamic-update-slice(bf16[512,768]{0,1:T(8,128)(2,1)S(1)} %dynamic_update_slice.58, bf16[32,768]{0,1:T(8,128)(2,1)S(1)} %copy.134, s32[]{:T(128)S(6)} %select_n.160, s32[]{:T(128)} %constant.133.clone.1) | dynamic-update-slice | bytes 98308 | tf_op jit(solution)/shard_map/dynamic_update_slice | solution.py:20
  151.6 2.9 %dynamic_update_slice.61 = bf16[512,768]{0,1:T(8,128)(2,1)S(1)} dynamic-update-slice(bf16[512,768]{0,1:T(8,128)(2,1)S(1)} %dynamic_update_slice.60, bf16[32,768]{0,1:T(8,128)(2,1)S(1)} %copy.136, s32[]{:T(128)S(6)} %select_n.164, s32[]{:T(128)} %constant.133.clone.1) | dynamic-update-slice | bytes 98308 | tf_op jit(solution)/shard_map/dynamic_update_slice | solution.py:20
  155.4 2.9 %dynamic_update_slice.62 = bf16[512,768]{0,1:T(8,128)(2,1)S(1)} dynamic-update-slice(bf16[512,768]{0,1:T(8,128)(2,1)S(1)} %dynamic_update_slice.61, bf16[32,768]{0,1:T(8,128)(2,1)S(1)} %copy.137, s32[]{:T(128)S(6)} %select_n.166, s32[]{:T(128)} %constant.133.clone.1) | dynamic-update-slice | bytes 98308 | tf_op jit(solution)/shard_map/dynamic_update_slice | solution.py:20
  159.3 2.9 %dynamic_update_slice.63 = bf16[512,768]{0,1:T(8,128)(2,1)S(1)} dynamic-update-slice(bf16[512,768]{0,1:T(8,128)(2,1)S(1)} %dynamic_update_slice.62, bf16[32,768]{0,1:T(8,128)(2,1)S(1)} %copy.138, s32[]{:T(128)S(6)} %select_n.168, s32[]{:T(128)} %constant.133.clone.1) | dynamic-update-slice | bytes 98308 | tf_op jit(solution)/shard_map/dynamic_update_slice | solution.py:20
  162.2 3.3 %fusion.9 = bf16[2,4,64,6,128]{4,2,3,1,0:T(8,128)(2,1)S(1)} fusion(f32[2,4,6,64,128]{4,3,2,1,0:T(8,128)} %fusion.14, bf16[512,6,128,1,1]{0,2,1,4,3:T(8,128)(2,1)S(1)} %bitcast.78, bf16[2,4,6,64,512]{4,3,1,0,2:T(8,128)(2,1)} %get-tuple-element.8, f32[2,4,64,6]{2,3,1,0:T(8,128)S(1)} %copy-done.22, f32[2,4,64,6]{2,3,1,0:T(8,128)S(1)} %copy-done.23), kind=kOutput, calls=%fused_computation.15 | convolution fusion | flops 404226048 | bytes 6316032 | tf_op jit(solution)/shard_map/fnhqk,khd->fnhqd/dot_general | solution.py:106
  (128 shorter events, 55.2 us)
Async XLA Ops:
  0.0 169.1 %copy-start = (bf16[768,1536]{1,0:T(8,128)(2,1)S(1)}, bf16[768,1536]{1,0:T(8,128)(2,1)}, u32[]{:S(2)}) copy-start(bf16[768,1536]{1,0:T(8,128)(2,1)} %param.13) | copy-start | bytes 7077892
  9.1 7.3 %collective-permute-start = (bf16[32,768]{1,0:T(8,128)(2,1)S(1)}, bf16[32,768]{1,0:T(8,128)(2,1)S(1)}, u32[]{:S(2)}, u32[]{:S(2)}) collective-permute-start(bf16[32,768]{1,0:T(8,128)(2,1)S(1)} %convert_element_type.64), channel_id=1, source_target_pairs={{0,1},{1,2},{2,3},{3,4},{4,5},{5,6},{6,7},{7,8},{8,9},{9,10},{10,1... | collective-permute-start | bytes 147464 | tf_op jit(solution)/shard_map/ppermute | solution.py:19
  16.4 6.2 %collective-permute-start.1 = (bf16[32,768]{1,0:T(8,128)(2,1)S(1)}, bf16[32,768]{1,0:T(8,128)(2,1)S(1)}, u32[]{:S(2)}, u32[]{:S(2)}) collective-permute-start(bf16[32,768]{1,0:T(8,128)(2,1)S(1)} %collective-permute-done), channel_id=1, source_target_pairs={{0,1},{1,2},{2,3},{3,4},{4,5},{5,6},{6,7},{7,8},{8,9},{9,10},{10,1... | collective-permute-start | bytes 147464 | tf_op jit(solution)/shard_map/ppermute | solution.py:19
  22.6 6.2 %collective-permute-start.2 = (bf16[32,768]{1,0:T(8,128)(2,1)S(1)}, bf16[32,768]{1,0:T(8,128)(2,1)S(1)}, u32[]{:S(2)}, u32[]{:S(2)}) collective-permute-start(bf16[32,768]{1,0:T(8,128)(2,1)S(1)} %collective-permute-done.1), channel_id=1, source_target_pairs={{0,1},{1,2},{2,3},{3,4},{4,5},{5,6},{6,7},{7,8},{8,9},{9,10},{10,1... | collective-permute-start | bytes 147464 | tf_op jit(solution)/shard_map/ppermute | solution.py:19
  25.0 37.8 %copy-start.24 = (s32[32]{0:T(128)S(1)}, s32[32]{0:T(128)}, u32[]{:S(2)}) copy-start(s32[32]{0:T(128)} %param.8) | copy-start | bytes 388
  28.8 6.2 %collective-permute-start.3 = (bf16[32,768]{1,0:T(8,128)(2,1)S(1)}, bf16[32,768]{1,0:T(8,128)(2,1)S(1)}, u32[]{:S(2)}, u32[]{:S(2)}) collective-permute-start(bf16[32,768]{1,0:T(8,128)(2,1)S(1)} %collective-permute-done.2), channel_id=1, source_target_pairs={{0,1},{1,2},{2,3},{3,4},{4,5},{5,6},{6,7},{7,8},{8,9},{9,10},{10,1... | collective-permute-start | bytes 147464 | tf_op jit(solution)/shard_map/ppermute | solution.py:19
  35.0 34.1 %copy-start.6 = (bf16[32,768]{1,0:T(8,128)(2,1)}, bf16[32,768]{1,0:T(8,128)(2,1)S(1)}, u32[]{:S(2)}) copy-start(bf16[32,768]{1,0:T(8,128)(2,1)S(1)} %collective-permute-done.3) | copy-start | bytes 147460
  35.0 21.5 %collective-permute-start.4 = (bf16[32,768]{1,0:T(8,128)(2,1)S(1)}, bf16[32,768]{1,0:T(8,128)(2,1)S(1)}, u32[]{:S(2)}, u32[]{:S(2)}) collective-permute-start(bf16[32,768]{1,0:T(8,128)(2,1)S(1)} %collective-permute-done.3), channel_id=1, source_target_pairs={{0,1},{1,2},{2,3},{3,4},{4,5},{5,6},{6,7},{7,8},{8,9},{9,10},{10,1... | collective-permute-start | bytes 147464 | tf_op jit(solution)/shard_map/ppermute | solution.py:19
  56.6 6.2 %collective-permute-start.5 = (bf16[32,768]{1,0:T(8,128)(2,1)S(1)}, bf16[32,768]{1,0:T(8,128)(2,1)S(1)}, u32[]{:S(2)}, u32[]{:S(2)}) collective-permute-start(bf16[32,768]{1,0:T(8,128)(2,1)S(1)} %collective-permute-done.4), channel_id=1, source_target_pairs={{0,1},{1,2},{2,3},{3,4},{4,5},{5,6},{6,7},{7,8},{8,9},{9,10},{10,1... | collective-permute-start | bytes 147464 | tf_op jit(solution)/shard_map/ppermute | solution.py:19
  62.8 6.2 %collective-permute-start.6 = (bf16[32,768]{1,0:T(8,128)(2,1)S(1)}, bf16[32,768]{1,0:T(8,128)(2,1)S(1)}, u32[]{:S(2)}, u32[]{:S(2)}) collective-permute-start(bf16[32,768]{1,0:T(8,128)(2,1)S(1)} %collective-permute-done.5), channel_id=1, source_target_pairs={{0,1},{1,2},{2,3},{3,4},{4,5},{5,6},{6,7},{7,8},{8,9},{9,10},{10,1... | collective-permute-start | bytes 147464 | tf_op jit(solution)/shard_map/ppermute | solution.py:19
  69.0 6.2 %collective-permute-start.7 = (bf16[32,768]{1,0:T(8,128)(2,1)S(1)}, bf16[32,768]{1,0:T(8,128)(2,1)S(1)}, u32[]{:S(2)}, u32[]{:S(2)}) collective-permute-start(bf16[32,768]{1,0:T(8,128)(2,1)S(1)} %collective-permute-done.6), channel_id=1, source_target_pairs={{0,1},{1,2},{2,3},{3,4},{4,5},{5,6},{6,7},{7,8},{8,9},{9,10},{10,1... | collective-permute-start | bytes 147464 | tf_op jit(solution)/shard_map/ppermute | solution.py:19
  75.2 6.2 %collective-permute-start.8 = (bf16[32,768]{1,0:T(8,128)(2,1)S(1)}, bf16[32,768]{1,0:T(8,128)(2,1)S(1)}, u32[]{:S(2)}, u32[]{:S(2)}) collective-permute-start(bf16[32,768]{1,0:T(8,128)(2,1)S(1)} %collective-permute-done.7), channel_id=1, source_target_pairs={{0,1},{1,2},{2,3},{3,4},{4,5},{5,6},{6,7},{7,8},{8,9},{9,10},{10,1... | collective-permute-start | bytes 147464 | tf_op jit(solution)/shard_map/ppermute | solution.py:19
  81.4 6.2 %collective-permute-start.9 = (bf16[32,768]{1,0:T(8,128)(2,1)S(1)}, bf16[32,768]{1,0:T(8,128)(2,1)S(1)}, u32[]{:S(2)}, u32[]{:S(2)}) collective-permute-start(bf16[32,768]{1,0:T(8,128)(2,1)S(1)} %collective-permute-done.8), channel_id=1, source_target_pairs={{0,1},{1,2},{2,3},{3,4},{4,5},{5,6},{6,7},{7,8},{8,9},{9,10},{10,1... | collective-permute-start | bytes 147464 | tf_op jit(solution)/shard_map/ppermute | solution.py:19
  87.6 6.2 %collective-permute-start.10 = (bf16[32,768]{1,0:T(8,128)(2,1)S(1)}, bf16[32,768]{1,0:T(8,128)(2,1)S(1)}, u32[]{:S(2)}, u32[]{:S(2)}) collective-permute-start(bf16[32,768]{1,0:T(8,128)(2,1)S(1)} %collective-permute-done.9), channel_id=1, source_target_pairs={{0,1},{1,2},{2,3},{3,4},{4,5},{5,6},{6,7},{7,8},{8,9},{9,10},{10,1... | collective-permute-start | bytes 147464 | tf_op jit(solution)/shard_map/ppermute | solution.py:19
  93.8 6.2 %collective-permute-start.11 = (bf16[32,768]{1,0:T(8,128)(2,1)S(1)}, bf16[32,768]{1,0:T(8,128)(2,1)S(1)}, u32[]{:S(2)}, u32[]{:S(2)}) collective-permute-start(bf16[32,768]{1,0:T(8,128)(2,1)S(1)} %collective-permute-done.10), channel_id=1, source_target_pairs={{0,1},{1,2},{2,3},{3,4},{4,5},{5,6},{6,7},{7,8},{8,9},{9,10},{10,1... | collective-permute-start | bytes 147464 | tf_op jit(solution)/shard_map/ppermute | solution.py:19
  100.1 6.2 %collective-permute-start.12 = (bf16[32,768]{1,0:T(8,128)(2,1)S(1)}, bf16[32,768]{1,0:T(8,128)(2,1)S(1)}, u32[]{:S(2)}, u32[]{:S(2)}) collective-permute-start(bf16[32,768]{1,0:T(8,128)(2,1)S(1)} %collective-permute-done.11), channel_id=1, source_target_pairs={{0,1},{1,2},{2,3},{3,4},{4,5},{5,6},{6,7},{7,8},{8,9},{9,10},{10,1... | collective-permute-start | bytes 147464 | tf_op jit(solution)/shard_map/ppermute | solution.py:19
  106.3 6.3 %collective-permute-start.13 = (bf16[32,768]{1,0:T(8,128)(2,1)S(1)}, bf16[32,768]{1,0:T(8,128)(2,1)}, u32[]{:S(2)}, u32[]{:S(2)}) collective-permute-start(bf16[32,768]{1,0:T(8,128)(2,1)S(1)} %collective-permute-done.12), channel_id=1, source_target_pairs={{0,1},{1,2},{2,3},{3,4},{4,5},{5,6},{6,7},{7,8},{8,9},{9,10},{10,1... | collective-permute-start | bytes 147464 | tf_op jit(solution)/shard_map/ppermute | solution.py:19
  112.6 45.7 %collective-permute-start.14 = (bf16[32,768]{1,0:T(8,128)(2,1)}, bf16[32,768]{1,0:T(8,128)(2,1)}, u32[]{:S(2)}, u32[]{:S(2)}) collective-permute-start(bf16[32,768]{1,0:T(8,128)(2,1)} %collective-permute-done.13), channel_id=1, source_target_pairs={{0,1},{1,2},{2,3},{3,4},{4,5},{5,6},{6,7},{7,8},{8,9},{9,10},{10,1... | collective-permute-start | bytes 147464 | tf_op jit(solution)/shard_map/ppermute | solution.py:19
  113.5 20.3 %copy-start.10 = (bf16[32,768]{1,0:T(8,128)(2,1)S(1)}, bf16[32,768]{1,0:T(8,128)(2,1)}, u32[]{:S(2)}) copy-start(bf16[32,768]{1,0:T(8,128)(2,1)} %copy-done.9) | copy-start | bytes 147460
  116.0 20.9 %copy-start.12 = (bf16[32,768]{1,0:T(8,128)(2,1)S(1)}, bf16[32,768]{1,0:T(8,128)(2,1)}, u32[]{:S(2)}) copy-start(bf16[32,768]{1,0:T(8,128)(2,1)} %copy-done.11) | copy-start | bytes 147460
  118.5 20.5 %copy-start.14 = (bf16[32,768]{1,0:T(8,128)(2,1)S(1)}, bf16[32,768]{1,0:T(8,128)(2,1)}, u32[]{:S(2)}) copy-start(bf16[32,768]{1,0:T(8,128)(2,1)} %copy-done.13) | copy-start | bytes 147460
  121.1 21.0 %copy-start.16 = (bf16[32,768]{1,0:T(8,128)(2,1)S(1)}, bf16[32,768]{1,0:T(8,128)(2,1)}, u32[]{:S(2)}) copy-start(bf16[32,768]{1,0:T(8,128)(2,1)} %copy-done.15) | copy-start | bytes 147460
  139.2 22.9 %copy-start.22 = (f32[2,4,64,6]{2,3,1,0:T(8,128)S(1)}, f32[2,4,64,6]{2,3,1,0:T(8,128)}, u32[]{:S(2)}) copy-start(f32[2,4,64,6]{2,3,1,0:T(8,128)} %get-tuple-element.5) | copy-start | bytes 36868
  142.3 19.9 %copy-start.23 = (f32[2,4,64,6]{2,3,1,0:T(8,128)S(1)}, f32[2,4,64,6]{2,3,1,0:T(8,128)}, u32[]{:S(2)}) copy-start(f32[2,4,64,6]{2,3,1,0:T(8,128)} %get-tuple-element.6) | copy-start | bytes 36868
  (18 other events, 161.2 us)
